TPU v7x, 32 devices: a whole 2x2x4 slice. The times are simulated.
32 devices in a mesh: ra: 8 (over z, y), dec: 4 (over x, core).
Axes of the slice: x: 2, y: 2, z: 4, core: 2. Of those that a mesh axis runs over, the one named last changes fastest.
Arguments:
- start_block: float32 [64, 512, 128], P('ra', 'dec'), may hold values from -6 to 6
- edge_blocks: float32 [64, 4, 4, 132, 128], P('ra', 'dec'), may hold values from -0.25 to 0.25
- block_offsets: int32 [64, 4, 4], P('ra', 'dec'), may hold values from 0 to 4
- degree_counts: int32 [64, 512], P('ra', 'dec'), may hold values from 4 to 12
Outputs:
- basis: float32 [64, 512, 128], P('ra', 'dec')
- rfactor: float32 [128, 128], replicated
All inputs are finite; a program needn't handle non-finite values.
Results may differ from a plain program's by a relative error of at most 0.0003.
Values sent between devices are 32-bit elements; how exact they have to be, the bound alone decides.
A program may use at most 64 MiB of HBM per device.

v0:
```python
import jax
import jax.numpy as jnp
from jax import lax
from jax.sharding import PartitionSpec as P


def padded(cells, sides, width, closed):
    for axis, dim in sides:
        count = lax.axis_size(axis)
        ends = count if closed else count - 1
        head = lax.slice_in_dim(cells, 0, width, axis=dim)
        tail = lax.slice_in_dim(cells, cells.shape[dim] - width, cells.shape[dim], axis=dim)
        cells = jnp.concatenate(
            [
                lax.ppermute(tail, axis, [(i, (i + 1) % count) for i in range(ends)]),
                cells,
                lax.ppermute(head, axis, [((i + 1) % count, i) for i in range(ends)]),
            ],
            axis=dim,
        )
    return cells


def extend_field(field):
    widened = padded(field, (("ra", 0),), 2, True)
    return padded(widened, (("dec", 1),), 2, False)


def apply_operator(field, local_blocks, local_offsets, degree_float):
    extended = extend_field(field)
    row_ids = lax.broadcasted_iota(jnp.int32, local_offsets.shape, 0)
    picked = extended[row_ids + local_offsets]
    coupled = jnp.einsum("ikqp,ikqc->ipc", local_blocks, picked, precision=lax.Precision.HIGHEST)
    return degree_float[:, :, None] * field - coupled


def lower_from_pairs(matrix):
    local_gram = jnp.dot(matrix.T, matrix, precision=lax.Precision.HIGHEST)
    return jnp.linalg.cholesky(lax.psum(local_gram, ("ra", "dec")))


def cholesky_pass(matrix):
    lower = lower_from_pairs(matrix)
    identity = jnp.eye(matrix.shape[1], dtype=matrix.dtype)
    inverse_lower = jax.scipy.linalg.solve_triangular(lower, identity, lower=True)
    ortho = jnp.dot(matrix, inverse_lower.T, precision=lax.Precision.HIGHEST)
    return (ortho, lower.T)


def on_device(start_block, edge_blocks, block_offsets, degree_counts):
    local_blocks = edge_blocks[:, 0]
    local_offsets = block_offsets[:, 0]
    degree_float = degree_counts.astype(jnp.float32)
    previous = start_block
    image = apply_operator(start_block, local_blocks, local_offsets, degree_float)
    current = (image - 8.0 * start_block) / 4.0
    for order_index in range(3):
        image = apply_operator(current, local_blocks, local_offsets, degree_float)
        following = 2.0 * (image - 8.0 * current) / 4.0 - previous
        previous = current
        current = following
    row_count, node_count, column_count = current.shape
    filtered = current.reshape(row_count * node_count, column_count)
    ortho_first, upper_first = cholesky_pass(filtered)
    ortho_second, upper_second = cholesky_pass(ortho_first)
    total_nodes = row_count * node_count * lax.axis_size("ra") * lax.axis_size("dec")
    scale = jnp.sqrt(jnp.asarray(total_nodes, dtype=jnp.float32))
    basis = (ortho_second * scale).reshape(row_count, node_count, column_count)
    rfactor = jnp.dot(upper_second, upper_first, precision=lax.Precision.HIGHEST) / scale
    return (basis, rfactor)


def solution(mesh):
    placed = (
        P("ra", "dec", None),
        P("ra", "dec", None, None, None),
        P("ra", "dec", None),
        P("ra", "dec"),
    )
    return jax.shard_map(
        on_device,
        mesh=mesh,
        in_specs=placed,
        out_specs=(P("ra", "dec", None), P()),
        check_vma=False,
    )
```

profile of v0, /device:TPU:1, one launch (start us, length us, event | category | flops | bytes accessed | tf_op | source)
XLA Modules:
  0.0 411.9 jit_solution(1014265469507738385)
XLA Ops:
  7.2 1.1 fusion.82
  8.4 5.2 %collective-permute-start.1 = (f32[2,128,128]{2,1,0:T(8,128)S(1)}, f32[2,128,128]{2,1,0:T(8,128)S(1)}, u32[]{:S(2)}, u32[]{:S(2)}) collective-permute-start(f32[2,128,128]{2,1,0:T(8,128)S(1)} %get-tuple-element.18), channel_id=1, source_target_pairs={{4,0},{8,4},{12,8},{16,12},{20,16},{24,20},{28,24},{0,28},{5,1},{9... | collective-permute-start | bytes 393224 | tf_op jit(solution)/shard_map/ppermute | solution.py:17
  13.5 0.7 compare_select_fusion
  14.4 5.7 %collective-permute-done = f32[2,128,128]{2,1,0:T(8,128)S(1)} collective-permute-done((f32[2,128,128]{2,1,0:T(8,128)S(1)}, f32[2,128,128]{2,1,0:T(8,128)S(1)}, u32[]{:S(2)}, u32[]{:S(2)}) %collective-permute-start) | collective-permute-done | bytes 131104 | tf_op jit(solution)/shard_map/ppermute | solution.py:15
  20.0 1.1 constant_dynamic-update-slice_fusion.1
  21.2 5.1 %collective-permute-start.2 = (f32[12,2,128]{2,1,0:T(2,128)S(1)}, f32[12,2,128]{2,1,0:T(2,128)S(1)}, u32[]{:S(2)}, u32[]{:S(2)}) collective-permute-start(f32[12,2,128]{2,1,0:T(2,128)S(1)} %get-tuple-element.10), channel_id=1, source_target_pairs={{0,1},{1,2},{2,3},{4,5},{5,6},{6,7},{8,9},{9,10},{10,11},{12,13},{... | collective-permute-start | bytes 36872 | tf_op jit(solution)/shard_map/ppermute | solution.py:15
  26.3 1.9 collective-permute-start.3
  28.2 0.7 convert_element_type.9
  28.9 2.4 collective-permute-done.3
  31.4 2.1 gather_fusion
  33.5 6.8 %broadcast_multiply_fusion = (f32[8,128,128]{2,1,0:T(8,128)S(1)}, f32[8,128,128]{2,1,0:T(8,128)}) fusion(f32[8,128,128]{2,1,0:T(8,128)S(1)} %copy-done.2, f32[8,4,132,128]{3,2,1,0:T(8,128)} %bitcast.98, f32[8,4,132,128]{3,1,2,0:T(4,128)S(1)} %bitcast.93, f32[8,128]{1,0:T(8,128)S(1)} %convert_element_type.9), kind=kOutput, calls=%fused_computation.37 | convolution fusion | flops 831127552 | bytes 5902336 | tf_op jit(solution)/shard_map/ikqp,ikqc->ipc/dot_general | solution.py:33
  40.4 4.1 %collective-permute-start.5 = (f32[2,128,128]{2,1,0:T(8,128)S(1)}, f32[2,128,128]{2,1,0:T(8,128)S(1)}, u32[]{:S(2)}, u32[]{:S(2)}) collective-permute-start(f32[2,128,128]{2,1,0:T(8,128)S(1)} %get-tuple-element.17), channel_id=1, source_target_pairs={{4,0},{8,4},{12,8},{16,12},{20,16},{24,20},{28,24},{0,28},{5,1},{9... | collective-permute-start | bytes 393224 | tf_op jit(solution)/shard_map/ppermute | solution.py:17
  44.5 2.4 collective-permute-done.4
  47.1 3.0 collective-permute-start.6
  50.0 1.9 collective-permute-start.7
  52.0 3.1 collective-permute-done.7
  55.1 2.1 gather_fusion.1
  57.2 6.1 %fusion.53 = f32[8,128,128]{2,1,0:T(8,128)S(1)} fusion(f32[8,128,128]{2,1,0:T(8,128)S(1)} %copy-done.2, f32[8,4,132,128]{3,2,1,0:T(8,128)} %bitcast.99, f32[8,4,132,128]{3,1,2,0:T(4,128)S(1)} %bitcast.96, f32[8,128,128]{2,1,0:T(8,128)} %get-tuple-element.21, f32[8,128]{1,0:T(8,128)S(1)} %broadcast_multiply_fusion.1), kind=kOutput, calls=%fused_computation.28 | convolution fusion | flops 831258624 | bytes 5902336 | tf_op jit(solution)/shard_map/ikqp,ikqc->ipc/dot_general | solution.py:33
  63.4 4.4 %collective-permute-start.9 = (f32[2,128,128]{2,1,0:T(8,128)S(1)}, f32[2,128,128]{2,1,0:T(8,128)S(1)}, u32[]{:S(2)}, u32[]{:S(2)}) collective-permute-start(f32[2,128,128]{2,1,0:T(8,128)S(1)} %get-tuple-element.15), channel_id=1, source_target_pairs={{4,0},{8,4},{12,8},{16,12},{20,16},{24,20},{28,24},{0,28},{5,1},{9... | collective-permute-start | bytes 393224 | tf_op jit(solution)/shard_map/ppermute | solution.py:17
  67.8 2.3 collective-permute-done.8
  70.1 3.0 collective-permute-start.10
  73.1 2.1 collective-permute-start.11
  75.3 2.9 collective-permute-done.11
  78.2 2.1 gather_fusion.2
  80.3 6.1 %fusion.41 = f32[8,128,128]{2,1,0:T(8,128)S(1)} fusion(f32[8,4,132,128]{3,2,1,0:T(8,128)} %bitcast.100, f32[8,4,132,128]{3,1,2,0:T(4,128)S(1)} %bitcast.95, f32[8,128,128]{2,1,0:T(8,128)S(1)} %fusion.53, f32[8,128]{1,0:T(8,128)S(1)} %convert_element_type.9, f32[8,128,128]{2,1,0:T(8,128)} %get-tuple-element.21), kind=kOutput, calls=%fused_computation.24 | convolution fusion | flops 831389696 | bytes 5902336 | tf_op jit(solution)/shard_map/ikqp,ikqc->ipc/dot_general | solution.py:33
  86.5 4.4 %collective-permute-start.13 = (f32[2,128,128]{2,1,0:T(8,128)S(1)}, f32[2,128,128]{2,1,0:T(8,128)S(1)}, u32[]{:S(2)}, u32[]{:S(2)}) collective-permute-start(f32[2,128,128]{2,1,0:T(8,128)S(1)} %get-tuple-element.13), channel_id=1, source_target_pairs={{4,0},{8,4},{12,8},{16,12},{20,16},{24,20},{28,24},{0,28},{5,1},{9... | collective-permute-start | bytes 393224 | tf_op jit(solution)/shard_map/ppermute | solution.py:17
  90.9 2.3 collective-permute-done.12
  93.2 3.1 collective-permute-start.14
  96.3 1.9 collective-permute-start.15
  98.2 3.1 collective-permute-done.15
  101.4 2.1 gather_fusion.3
  103.5 6.1 %fusion.29 = f32[8,128,128]{2,1,0:T(8,128)S(1)} fusion(f32[8,128,128]{2,1,0:T(8,128)S(1)} %fusion.53, f32[8,4,132,128]{3,2,1,0:T(8,128)} %bitcast.97, f32[8,4,132,128]{3,1,2,0:T(4,128)S(1)} %bitcast.94, f32[8,128,128]{2,1,0:T(8,128)} %copy-done.1, f32[8,128]{1,0:T(8,128)S(1)} %convert_element_type.9), kind=kOutput, calls=%fused_computation.20 | convolution fusion | flops 831258624 | bytes 5902336 | tf_op jit(solution)/shard_map/ikqp,ikqc->ipc/dot_general | solution.py:33
  109.5 1.6 convolution_bitcast_fusion
  111.5 119.0 %all-reduce.3.cloned.1.call-done = f32[128,128]{0,1:T(8,128)} async-done(((f32[128,128]{0,1:T(8,128)}), f32[128,128]{0,1:T(8,128)}) %all-reduce.3.cloned.1.call-update) | async-done | bytes 65552 | tf_op jit(solution)/shard_map/psum | solution.py:39
  230.5 0.9 copy.23
  231.4 0.9 fusion.69
  232.2 11.7 %cholesky.44 = f32[128,128]{1,0:T(8,128)S(1)} custom-call(f32[128,128]{1,0:T(8,128)S(1)} %fusion.69), custom_call_target="Cholesky" | custom-call | tf_op jit(solution)/shard_map/jit(cholesky)/cholesky | solution.py:39
  244.0 0.6 compare_reduce_fusion.1
  244.6 0.7 select_bitcast_fusion.1
  245.3 9.8 %custom-call.6 = f32[1,128,128]{1,2,0:T(8,128)S(1)} custom-call(f32[1,128,128]{2,1,0:T(8,128)S(1)} %select_bitcast_fusion.1), custom_call_target="InvertDiagBlocksLowerTriangular" | custom-call | tf_op jit(solution)/shard_map/jit(_solve_triangular)/triangular_solve | solution.py:45
  256.0 1.6 fusion.84
  257.6 118.5 %all-reduce.5.cloned.1.call-done = f32[128,128]{0,1:T(8,128)} async-done(((f32[128,128]{0,1:T(8,128)}), f32[128,128]{0,1:T(8,128)}) %all-reduce.5.cloned.1.call-update) | async-done | bytes 65552 | tf_op jit(solution)/shard_map/psum | solution.py:39
  376.1 0.9 copy.25
  377.1 0.9 fusion.67
  377.9 11.7 %cholesky.55 = f32[128,128]{1,0:T(8,128)S(1)} custom-call(f32[128,128]{1,0:T(8,128)S(1)} %fusion.67), custom_call_target="Cholesky" | custom-call | tf_op jit(solution)/shard_map/jit(cholesky)/cholesky | solution.py:39
  390.3 2.1 convolution_multiply_fusion.1
  393.0 10.0 %custom-call.7 = f32[1,128,128]{1,2,0:T(8,128)S(1)} custom-call(f32[1,128,128]{2,1,0:T(8,128)S(1)} %select_bitcast_fusion), custom_call_target="InvertDiagBlocksLowerTriangular" | custom-call | tf_op jit(solution)/shard_map/jit(_solve_triangular)/triangular_solve | solution.py:45
  403.3 1.4 convolution_multiply_fusion
  (48 shorter events, 3.7 us)
Async XLA Ops:
  7.2 26.3 %copy-start = (f32[8,1,4,132,128]{4,2,3,1,0:T(4,128)S(1)}, f32[8,1,4,132,128]{4,2,3,1,0:T(4,128)}, u32[]{:S(2)}) copy-start(f32[8,1,4,132,128]{4,2,3,1,0:T(4,128)} %param.8) | copy-start | bytes 6488068
  7.2 223.3 %all-reduce.3.cloned.1.call-start = ((), (), s32[]{:S(2)}) async-start(), calls=%async_computation | async-start | bytes 131072 | tf_op jit(solution)/shard_map/psum | solution.py:39
  8.4 12.8 %collective-permute-start.1 = (f32[2,128,128]{2,1,0:T(8,128)S(1)}, f32[2,128,128]{2,1,0:T(8,128)S(1)}, u32[]{:S(2)}, u32[]{:S(2)}) collective-permute-start(f32[2,128,128]{2,1,0:T(8,128)S(1)} %get-tuple-element.18), channel_id=1, source_target_pairs={{4,0},{8,4},{12,8},{16,12},{20,16},{24,20},{28,24},{0,28},{5,1},{9... | collective-permute-start | bytes 393224 | tf_op jit(solution)/shard_map/ppermute | solution.py:17
  13.5 6.5 %collective-permute-start = (f32[2,128,128]{2,1,0:T(8,128)S(1)}, f32[2,128,128]{2,1,0:T(8,128)S(1)}, u32[]{:S(2)}, u32[]{:S(2)}) collective-permute-start(f32[2,128,128]{2,1,0:T(8,128)S(1)} %get-tuple-element.19), channel_id=1, source_target_pairs={{0,4},{4,8},{8,12},{12,16},{16,20},{20,24},{24,28},{28,0},{1,5},{5... | collective-permute-start | bytes 393224 | tf_op jit(solution)/shard_map/ppermute | solution.py:15
  21.2 7.8 %collective-permute-start.2 = (f32[12,2,128]{2,1,0:T(2,128)S(1)}, f32[12,2,128]{2,1,0:T(2,128)S(1)}, u32[]{:S(2)}, u32[]{:S(2)}) collective-permute-start(f32[12,2,128]{2,1,0:T(2,128)S(1)} %get-tuple-element.10), channel_id=1, source_target_pairs={{0,1},{1,2},{2,3},{4,5},{5,6},{6,7},{8,9},{9,10},{10,11},{12,13},{... | collective-permute-start | bytes 36872 | tf_op jit(solution)/shard_map/ppermute | solution.py:15
  26.3 5.0 %collective-permute-start.3 = (f32[12,2,128]{2,1,0:T(2,128)S(1)}, f32[12,2,128]{2,1,0:T(2,128)S(1)}, u32[]{:S(2)}, u32[]{:S(2)}) collective-permute-start(f32[12,2,128]{2,1,0:T(2,128)S(1)} %get-tuple-element.11), channel_id=1, source_target_pairs={{1,0},{2,1},{3,2},{5,4},{6,5},{7,6},{9,8},{10,9},{11,10},{13,12},{... | collective-permute-start | bytes 36872 | tf_op jit(solution)/shard_map/ppermute | solution.py:17
  31.4 2.1 copy-start.2
  33.5 18.5 %copy-start.3 = (s32[8,128]{1,0:T(8,128)S(1)}, s32[8,128]{1,0:T(8,128)}, u32[]{:S(2)}) copy-start(s32[8,128]{1,0:T(8,128)} %param.10) | copy-start | bytes 12292
  40.3 6.6 %collective-permute-start.4 = (f32[2,128,128]{2,1,0:T(8,128)S(1)}, f32[2,128,128]{2,1,0:T(8,128)S(1)}, u32[]{:S(2)}, u32[]{:S(2)}) collective-permute-start(f32[2,128,128]{2,1,0:T(8,128)S(1)} %get-tuple-element.16), channel_id=1, source_target_pairs={{0,4},{4,8},{8,12},{12,16},{16,20},{20,24},{24,28},{28,0},{1,5},{5... | collective-permute-start | bytes 393224 | tf_op jit(solution)/shard_map/ppermute | solution.py:15
  40.4 6.7 %collective-permute-start.5 = (f32[2,128,128]{2,1,0:T(8,128)S(1)}, f32[2,128,128]{2,1,0:T(8,128)S(1)}, u32[]{:S(2)}, u32[]{:S(2)}) collective-permute-start(f32[2,128,128]{2,1,0:T(8,128)S(1)} %get-tuple-element.17), channel_id=1, source_target_pairs={{4,0},{8,4},{12,8},{16,12},{20,16},{24,20},{28,24},{0,28},{5,1},{9... | collective-permute-start | bytes 393224 | tf_op jit(solution)/shard_map/ppermute | solution.py:17
  47.1 4.9 %collective-permute-start.6 = (f32[12,2,128]{2,1,0:T(2,128)S(1)}, f32[12,2,128]{2,1,0:T(2,128)S(1)}, u32[]{:S(2)}, u32[]{:S(2)}) collective-permute-start(f32[12,2,128]{2,1,0:T(2,128)S(1)} %get-tuple-element.8), channel_id=1, source_target_pairs={{0,1},{1,2},{2,3},{4,5},{5,6},{6,7},{8,9},{9,10},{10,11},{12,13},{... | collective-permute-start | bytes 36872 | tf_op jit(solution)/shard_map/ppermute | solution.py:15
  50.0 5.0 %collective-permute-start.7 = (f32[12,2,128]{2,1,0:T(2,128)S(1)}, f32[12,2,128]{2,1,0:T(2,128)S(1)}, u32[]{:S(2)}, u32[]{:S(2)}) collective-permute-start(f32[12,2,128]{2,1,0:T(2,128)S(1)} %get-tuple-element.9), channel_id=1, source_target_pairs={{1,0},{2,1},{3,2},{5,4},{6,5},{7,6},{9,8},{10,9},{11,10},{13,12},{... | collective-permute-start | bytes 36872 | tf_op jit(solution)/shard_map/ppermute | solution.py:17
  63.3 6.8 %collective-permute-start.8 = (f32[2,128,128]{2,1,0:T(8,128)S(1)}, f32[2,128,128]{2,1,0:T(8,128)S(1)}, u32[]{:S(2)}, u32[]{:S(2)}) collective-permute-start(f32[2,128,128]{2,1,0:T(8,128)S(1)} %get-tuple-element.14), channel_id=1, source_target_pairs={{0,4},{4,8},{8,12},{12,16},{16,20},{20,24},{24,28},{28,0},{1,5},{5... | collective-permute-start | bytes 393224 | tf_op jit(solution)/shard_map/ppermute | solution.py:15
  63.4 6.7 %collective-permute-start.9 = (f32[2,128,128]{2,1,0:T(8,128)S(1)}, f32[2,128,128]{2,1,0:T(8,128)S(1)}, u32[]{:S(2)}, u32[]{:S(2)}) collective-permute-start(f32[2,128,128]{2,1,0:T(8,128)S(1)} %get-tuple-element.15), channel_id=1, source_target_pairs={{4,0},{8,4},{12,8},{16,12},{20,16},{24,20},{28,24},{0,28},{5,1},{9... | collective-permute-start | bytes 393224 | tf_op jit(solution)/shard_map/ppermute | solution.py:17
  70.1 5.1 %collective-permute-start.10 = (f32[12,2,128]{2,1,0:T(2,128)S(1)}, f32[12,2,128]{2,1,0:T(2,128)S(1)}, u32[]{:S(2)}, u32[]{:S(2)}) collective-permute-start(f32[12,2,128]{2,1,0:T(2,128)S(1)} %get-tuple-element.6), channel_id=1, source_target_pairs={{0,1},{1,2},{2,3},{4,5},{5,6},{6,7},{8,9},{9,10},{10,11},{12,13},{... | collective-permute-start | bytes 36872 | tf_op jit(solution)/shard_map/ppermute | solution.py:15
  73.1 5.0 %collective-permute-start.11 = (f32[12,2,128]{2,1,0:T(2,128)S(1)}, f32[12,2,128]{2,1,0:T(2,128)S(1)}, u32[]{:S(2)}, u32[]{:S(2)}) collective-permute-start(f32[12,2,128]{2,1,0:T(2,128)S(1)} %get-tuple-element.7), channel_id=1, source_target_pairs={{1,0},{2,1},{3,2},{5,4},{6,5},{7,6},{9,8},{10,9},{11,10},{13,12},{... | collective-permute-start | bytes 36872 | tf_op jit(solution)/shard_map/ppermute | solution.py:17
  86.4 14.9 %copy-start.1 = (f32[8,128,128]{2,1,0:T(8,128)}, f32[8,128,128]{2,1,0:T(8,128)S(1)}, u32[]{:S(2)}) copy-start(f32[8,128,128]{2,1,0:T(8,128)S(1)} %fusion.41) | copy-start | bytes 1572868
  86.4 6.7 %collective-permute-start.12 = (f32[2,128,128]{2,1,0:T(8,128)S(1)}, f32[2,128,128]{2,1,0:T(8,128)S(1)}, u32[]{:S(2)}, u32[]{:S(2)}) collective-permute-start(f32[2,128,128]{2,1,0:T(8,128)S(1)} %get-tuple-element.12), channel_id=1, source_target_pairs={{0,4},{4,8},{8,12},{12,16},{16,20},{20,24},{24,28},{28,0},{1,5},{5... | collective-permute-start | bytes 393224 | tf_op jit(solution)/shard_map/ppermute | solution.py:15
  86.5 6.7 %collective-permute-start.13 = (f32[2,128,128]{2,1,0:T(8,128)S(1)}, f32[2,128,128]{2,1,0:T(8,128)S(1)}, u32[]{:S(2)}, u32[]{:S(2)}) collective-permute-start(f32[2,128,128]{2,1,0:T(8,128)S(1)} %get-tuple-element.13), channel_id=1, source_target_pairs={{4,0},{8,4},{12,8},{16,12},{20,16},{24,20},{28,24},{0,28},{5,1},{9... | collective-permute-start | bytes 393224 | tf_op jit(solution)/shard_map/ppermute | solution.py:17
  93.2 5.0 %collective-permute-start.14 = (f32[12,2,128]{2,1,0:T(2,128)S(1)}, f32[12,2,128]{2,1,0:T(2,128)S(1)}, u32[]{:S(2)}, u32[]{:S(2)}) collective-permute-start(f32[12,2,128]{2,1,0:T(2,128)S(1)} %get-tuple-element.4), channel_id=1, source_target_pairs={{0,1},{1,2},{2,3},{4,5},{5,6},{6,7},{8,9},{9,10},{10,11},{12,13},{... | collective-permute-start | bytes 36872 | tf_op jit(solution)/shard_map/ppermute | solution.py:15
  96.3 5.0 %collective-permute-start.15 = (f32[12,2,128]{2,1,0:T(2,128)S(1)}, f32[12,2,128]{2,1,0:T(2,128)S(1)}, u32[]{:S(2)}, u32[]{:S(2)}) collective-permute-start(f32[12,2,128]{2,1,0:T(2,128)S(1)} %get-tuple-element.5), channel_id=1, source_target_pairs={{1,0},{2,1},{3,2},{5,4},{6,5},{7,6},{9,8},{10,9},{11,10},{13,12},{... | collective-permute-start | bytes 36872 | tf_op jit(solution)/shard_map/ppermute | solution.py:17
  111.2 264.9 %all-reduce.5.cloned.1.call-start = ((), (), s32[]{:S(2)}) async-start(), calls=%async_computation.1 | async-start | bytes 131072 | tf_op jit(solution)/shard_map/psum | solution.py:39
Sparse Core Ops, SparseCore 0:
  111.3 119.0 all-reduce.2
  257.8 118.3 all-reduce.4
where the time goes:
time: 420 us; the launch traced here: 412 us
  waiting for transfers between devices  262 us (62%)
  other arithmetic  49.2 us (12%)
  starting transfers between devices  40.6 us (10%)
  matrix products  32.9 us (8%)
  between operations  14.8 us (4%)
  local copies, waits for them, and re-layouts  12.6 us (3%)
    psum x2, waiting for transfers between devices, lower_from_pairs(): return jnp.linalg.cholesky(lax.psum(local_gram, ('ra', 'dec')))  237 us
    ppermute x8, starting transfers between devices, padded(): lax.ppermute(head, axis, [((i + 1) % count, i) for i in range(ends)])  26 us
    dot_general x4, matrix products, apply_operator(): jnp.einsum('ikqp,ikqc->ipc', local_blocks, picked, precision=lax.Precisio...  25 us
    another operation x6, other arithmetic, lower_from_pairs(): return jnp.linalg.cholesky(lax.psum(local_gram, ('ra', 'dec')))  24.7 us
    another operation x4, other arithmetic, cholesky_pass(): jax.scipy.linalg.solve_triangular(lower, identity, lower=True)  21.1 us
    ppermute x8, starting transfers between devices, padded(): lax.ppermute(tail, axis, [(i, (i + 1) % count) for i in range(ends)])  14.4 us
    ppermute x8, waiting for transfers between devices, padded(): lax.ppermute(tail, axis, [(i, (i + 1) % count) for i in range(ends)])  12.7 us
    ppermute x8, waiting for transfers between devices, padded(): lax.ppermute(head, axis, [((i + 1) % count, i) for i in range(ends)])  11.5 us
  transfers between devices with their start and end apart: 18, of which 11 were waited for; matrix products, arithmetic and copies ran while one was open for 1% of the time, Pallas kernels for 0%

commit v1 on v0

v1 whole, which is shorter than its diff:
```python
import functools

import jax
import jax.numpy as jnp
from jax import lax
from jax.experimental import pallas as pl
from jax.experimental.pallas import tpu as pltpu
from jax.sharding import PartitionSpec as P

MESH = pl.DeviceIdType.MESH
F32 = jnp.float32
BF16 = jnp.bfloat16
STEPS = 4
HALO = 64


def three_parts(value):
    first = value.astype(BF16)
    rest = value - first.astype(F32)
    second = rest.astype(BF16)
    third = (rest - second.astype(F32)).astype(BF16)
    return first, second, third


def filter_kernel(
    ra_count, dec_count, offsets, start, edges, degrees, out,
    fields, low, high, left, right, wide, thin, wide_halo, thin_halo, edge_pair, edge_third, degree_cols,
    send_sem, recv_sem,
):
    rows = start.shape[0]
    ra = lax.axis_index("ra")
    dec = lax.axis_index("dec")
    up = lax.rem(ra + 1, ra_count)
    down = lax.rem(ra + ra_count - 1, ra_count)
    has_left = dec > 0
    has_right = dec < dec_count - 1

    barrier = pltpu.get_barrier_semaphore()

    def greet(r, d):
        pl.semaphore_signal(barrier, inc=1, device_id=(r, d), device_id_type=MESH)

    greet(up, dec)
    greet(down, dec)

    @pl.when(has_left)
    def _():
        for r in (up, down, ra):
            greet(r, dec - 1)

    @pl.when(has_right)
    def _():
        for r in (up, down, ra):
            greet(r, dec + 1)

    pl.semaphore_wait(barrier, 2 + 3 * jnp.where(has_left, 1, 0) + 3 * jnp.where(has_right, 1, 0))

    def copy(version, slot, source, target, r, d):
        return pltpu.make_async_remote_copy(
            src_ref=source, dst_ref=target, send_sem=send_sem.at[version, slot], recv_sem=recv_sem.at[version, slot],
            device_id=(r, d), device_id_type=MESH,
        )

    def copies(version):
        field = start if version == 0 else fields.at[version - 1]
        first, last = pl.ds(0, 2), pl.ds(rows - 2, 2)
        head, tail = pl.ds(0, 8), pl.ds(120, 8)
        top, bottom, middle = pl.ds(0, 2), pl.ds(rows + 2, 2), pl.ds(2, rows)
        to_right, to_left = left.at[version], right.at[version]
        ring = [
            copy(version, 0, field.at[last], low.at[version], up, dec),
            copy(version, 1, field.at[first], high.at[version], down, dec),
        ]
        rightward = [
            copy(version, 2, field.at[last, tail], to_right.at[top], up, dec + 1),
            copy(version, 3, field.at[first, tail], to_right.at[bottom], down, dec + 1),
            copy(version, 4, field.at[:, tail], to_right.at[middle], ra, dec + 1),
        ]
        leftward = [
            copy(version, 5, field.at[last, head], to_left.at[top], up, dec - 1),
            copy(version, 6, field.at[first, head], to_left.at[bottom], down, dec - 1),
            copy(version, 7, field.at[:, head], to_left.at[middle], ra, dec - 1),
        ]
        return ring, rightward, leftward

    def start_edges(version):
        ring, rightward, leftward = copies(version)
        for c in ring:
            c.start()

        @pl.when(has_right)
        def _():
            for c in rightward[:2]:
                c.start()

        @pl.when(has_left)
        def _():
            for c in leftward[:2]:
                c.start()

    def start_middle(version):
        _, rightward, leftward = copies(version)

        @pl.when(has_right)
        def _():
            rightward[2].start()

        @pl.when(has_left)
        def _():
            leftward[2].start()

    def receive(version):
        ring, rightward, leftward = copies(version)
        for c in ring:
            c.wait_recv()

        @pl.when(has_left)
        def _():
            for c in rightward:
                c.wait_recv()

        @pl.when(has_right)
        def _():
            for c in leftward:
                c.wait_recv()

    def finish_sends(version):
        ring, rightward, leftward = copies(version)
        for c in ring:
            c.wait_send()

        @pl.when(has_right)
        def _():
            for c in rightward:
                c.wait_send()

        @pl.when(has_left)
        def _():
            for c in leftward:
                c.wait_send()

    def put(turn, place, value):
        first, second, third = three_parts(value)
        wide[turn, place, :, 0:128] = first
        wide[turn, place, :, 128:256] = second
        thin[turn, place] = third

    start_edges(0)
    start_middle(0)

    for version in range(STEPS):
        @pl.when(dec == 0)
        def _():
            left[version] = jnp.zeros_like(left[version])

        @pl.when(dec == dec_count - 1)
        def _():
            right[version] = jnp.zeros_like(right[version])

    turned = jnp.transpose(degrees[...].astype(F32))
    for row in range(rows):
        degree_cols[row] = jnp.broadcast_to(turned[:, row : row + 1], (128, 128)) - 8.0

    def prepare(row, carry):
        put(0, row + 2, start[row])
        pieces = [edges[row, k, 2:130, :].T for k in range(4)]
        blank = jnp.zeros((6, 128), F32)
        tips = []
        for k in range(4):
            tips += [blank, edges[row, k, 0:2, :], edges[row, k, 130:132, :], blank]
        pieces.append(jnp.concatenate(tips, axis=0).T)
        turned_edges = jnp.concatenate(pieces, axis=1)
        first, second, third = three_parts(turned_edges)
        edge_pair[row, 0:128] = first
        edge_pair[row, 128:256] = second
        edge_third[row] = third
        return carry

    lax.fori_loop(0, rows, prepare, 0)

    def one_row(version, row):
        turn = version % 2
        places = [row + offsets[row, k] for k in range(4)]
        both = jnp.concatenate([wide[turn, p] for p in places] + [wide_halo[p] for p in places], axis=0)
        last = jnp.concatenate([thin[turn, p] for p in places] + [thin_halo[p] for p in places], axis=0)
        pair = edge_pair[row]
        square = jnp.dot(pair, both, preferred_element_type=F32)
        small = jnp.dot(pair[0:128], last, preferred_element_type=F32) + jnp.dot(
            edge_third[row], both[:, 0:128], preferred_element_type=F32
        )
        small = square[128:256, 128:256] + small
        coupled = square[0:128, 0:128] + ((square[0:128, 128:256] + square[128:256, 0:128]) + small)
        field = start[row] if version == 0 else fields[version - 1, row]
        image = degree_cols[row] * field - coupled
        if version == 0:
            return image * 0.25
        before = start[row] if version == 1 else fields[version - 2, row]
        return image * 0.5 - before

    def run_row(version, row):
        value = one_row(version, row)
        if version == STEPS - 1:
            out[row] = value
        else:
            fields[version, row] = value
            put((version + 1) % 2, row + 2, value)

    for version in range(STEPS):
        turn = version % 2
        receive(version)
        for i in range(2):
            put(turn, i, low[version, i])
            put(turn, rows + 2 + i, high[version, i])

        def halo(place, carry):
            tips = jnp.concatenate([left[version, place], right[version, place]], axis=0)
            first, second, third = three_parts(tips)
            wide_halo[place, :, 0:128] = first
            wide_halo[place, :, 128:256] = second
            thin_halo[place] = third
            return carry

        lax.fori_loop(0, rows + 4, halo, 0)

        def boundary(i, carry):
            run_row(version, i + (rows - 4) * (i // 2))
            return carry

        def interior(i, carry):
            run_row(version, i + 2)
            return carry

        lax.fori_loop(0, 4, boundary, 0)
        if version < STEPS - 1:
            start_edges(version + 1)
        lax.fori_loop(0, rows - 4, interior, 0)
        if version < STEPS - 1:
            start_middle(version + 1)

    for version in range(STEPS):
        finish_sends(version)


def filtered_field(start_block, edges, offsets, degrees):
    rows = start_block.shape[0]
    vmem = pl.BlockSpec(memory_space=pltpu.VMEM)
    depth = 4 * 128 + HALO
    return pl.pallas_call(
        functools.partial(filter_kernel, lax.axis_size("ra"), lax.axis_size("dec")),
        out_shape=jax.ShapeDtypeStruct(start_block.shape, F32),
        in_specs=[pl.BlockSpec(memory_space=pltpu.SMEM), vmem, vmem, vmem],
        out_specs=vmem,
        scratch_shapes=[
            pltpu.VMEM((STEPS - 1, rows, 128, 128), F32),
            pltpu.VMEM((STEPS, 2, 128, 128), F32),
            pltpu.VMEM((STEPS, 2, 128, 128), F32),
            pltpu.VMEM((STEPS, rows + 4, 8, 128), F32),
            pltpu.VMEM((STEPS, rows + 4, 8, 128), F32),
            pltpu.VMEM((2, rows + 4, 128, 256), BF16),
            pltpu.VMEM((2, rows + 4, 128, 128), BF16),
            pltpu.VMEM((rows + 4, 16, 256), BF16),
            pltpu.VMEM((rows + 4, 16, 128), BF16),
            pltpu.VMEM((rows, 256, depth), BF16),
            pltpu.VMEM((rows, 128, depth), BF16),
            pltpu.VMEM((rows, 128, 128), F32),
            pltpu.SemaphoreType.DMA((STEPS, 8)),
            pltpu.SemaphoreType.DMA((STEPS, 8)),
        ],
        compiler_params=pltpu.CompilerParams(collective_id=0, has_side_effects=True, vmem_limit_bytes=48 * 2**20),
        name="filter",
    )(offsets, start_block, edges, degrees)


def gram_kernel(ra_count, dec_count, matrix, total, sums, came, send_sem, recv_sem):
    ra = lax.axis_index("ra")
    dec = lax.axis_index("dec")
    partners = []
    for bit in range(dec_count.bit_length() - 1):
        step = 2**bit
        partners.append((ra, dec + step - 2 * step * lax.rem(dec // step, 2)))
    for bit in range(ra_count.bit_length() - 1):
        step = 2**bit
        partners.append((ra + step - 2 * step * lax.rem(ra // step, 2), dec))
    barrier = pltpu.get_barrier_semaphore()
    for partner in partners:
        pl.semaphore_signal(barrier, inc=1, device_id=partner, device_id_type=MESH)
    local = lax.dot_general(
        matrix[...], matrix[...], (((0,), (0,)), ((), ())), precision=lax.Precision.HIGHEST, preferred_element_type=F32
    )
    pl.semaphore_wait(barrier, len(partners))
    for level, partner in enumerate(partners):
        sums[level] = local
        move = pltpu.make_async_remote_copy(
            src_ref=sums.at[level], dst_ref=came.at[level], send_sem=send_sem.at[level], recv_sem=recv_sem.at[level],
            device_id=partner, device_id_type=MESH,
        )
        move.start()
        move.wait()
        local = local + came[level]
    total[...] = local


def whole_gram(matrix):
    vmem = pl.BlockSpec(memory_space=pltpu.VMEM)
    levels = lax.axis_size(("ra", "dec")).bit_length() - 1
    return pl.pallas_call(
        functools.partial(gram_kernel, lax.axis_size("ra"), lax.axis_size("dec")),
        out_shape=jax.ShapeDtypeStruct((128, 128), F32),
        in_specs=[vmem],
        out_specs=vmem,
        scratch_shapes=[
            pltpu.VMEM((levels, 128, 128), F32),
            pltpu.VMEM((levels, 128, 128), F32),
            pltpu.SemaphoreType.DMA((levels,)),
            pltpu.SemaphoreType.DMA((levels,)),
        ],
        compiler_params=pltpu.CompilerParams(collective_id=1, has_side_effects=True),
        name="gram",
    )(matrix)


def cholesky_pass(matrix):
    lower = jnp.linalg.cholesky(whole_gram(matrix))
    identity = jnp.eye(matrix.shape[1], dtype=matrix.dtype)
    inverse_lower = jax.scipy.linalg.solve_triangular(lower, identity, lower=True)
    ortho = jnp.dot(matrix, inverse_lower.T, precision=lax.Precision.HIGHEST)
    return (ortho, lower.T)


def on_device(start_block, edge_blocks, block_offsets, degree_counts):
    current = filtered_field(start_block, edge_blocks[:, 0], block_offsets[:, 0], degree_counts)
    row_count, node_count, column_count = current.shape
    filtered = current.reshape(row_count * node_count, column_count)
    ortho_first, upper_first = cholesky_pass(filtered)
    ortho_second, upper_second = cholesky_pass(ortho_first)
    total_nodes = row_count * node_count * lax.axis_size("ra") * lax.axis_size("dec")
    scale = jnp.sqrt(jnp.asarray(total_nodes, dtype=jnp.float32))
    basis = (ortho_second * scale).reshape(row_count, node_count, column_count)
    rfactor = jnp.dot(upper_second, upper_first, precision=lax.Precision.HIGHEST) / scale
    return (basis, rfactor)


def solution(mesh):
    placed = (
        P("ra", "dec", None),
        P("ra", "dec", None, None, None),
        P("ra", "dec", None),
        P("ra", "dec"),
    )
    return jax.shard_map(
        on_device,
        mesh=mesh,
        in_specs=placed,
        out_specs=(P("ra", "dec", None), P()),
        check_vma=False,
    )
```

time: 420 us -> 144 us (0.34)
  the two profiles are of different devices: /device:TPU:1 before, /device:TPU:0 now
where the time goes in v1:
time: 144 us
  Pallas kernels  82.6 us (57%)
  other arithmetic  47.5 us (33%)
  matrix products  7.52 us (5%)
  local copies, waits for them, and re-layouts  5.23 us (4%)
    pallas_call x1, Pallas kernels, filtered_field(): pl.pallas_call(functools.partial(filter_kernel, lax.axis_size('ra'), lax....  45.8 us
    pallas_call x2, Pallas kernels, whole_gram(): pl.pallas_call(functools.partial(gram_kernel, lax.axis_size('ra'), lax.ax...  36.8 us
    another operation x6, other arithmetic, cholesky_pass(): lower = jnp.linalg.cholesky(whole_gram(matrix))  25 us
    another operation x4, other arithmetic, cholesky_pass(): jax.scipy.linalg.solve_triangular(lower, identity, lower=True)  20.8 us
    dot_general x2, matrix products, cholesky_pass(): ortho = jnp.dot(matrix, inverse_lower.T, precision=lax.Precision.HIGHEST)  4.83 us

profile of v1, /device:TPU:0, one launch (start us, length us, event | category | flops | bytes accessed | tf_op | source)
XLA Modules:
  0.0 143.6 jit_solution(5398028414920065947)
XLA Ops:
  0.6 0.0 copy-start.2
  0.6 0.0 copy-start.1
  0.6 0.8 copy.7.offsets
  1.5 1.8 %copy.11 = f32[8,1,4,132,128]{4,3,2,0,1:T(8,128)S(1)} copy(f32[8,1,4,132,128]{4,2,3,1,0:T(4,128)} %param.8) | data formatting | bytes 4325376 | tf_op args[1]
  3.2 0.0 copy-done.2
  3.2 0.0 copy-done.1
  3.2 45.8 %filter.1 = f32[8,128,128]{2,1,0:T(8,128)S(1)} custom-call(s32[8,4]{1,0:T(8,128)S(1)} %copy.7.offsets, f32[8,128,128]{2,1,0:T(8,128)S(1)} %copy-done.1, f32[8,4,132,128]{3,2,1,0:T(8,128)S(1)} %bitcast.28, s32[8,128]{1,0:T(8,128)S(1)} %copy-done.2), custom_call_target="tpu_custom_call" | custom-call | tf_op jit(solution)/shard_map/filter/pallas_call | solution.py:248
  49.0 0.0 copy-start
  49.1 0.8 copy-done
  49.8 19.2 %gram.2 = f32[128,128]{1,0:T(8,128)} custom-call(f32[1024,128]{1,0:T(8,128)} %bitcast.29), custom_call_target="tpu_custom_call" | custom-call | tf_op jit(solution)/shard_map/gram/pallas_call | solution.py:306
  69.0 0.9 copy.8
  70.0 0.9 fusion.7
  70.8 11.7 %cholesky.44 = f32[128,128]{1,0:T(8,128)S(1)} custom-call(f32[128,128]{1,0:T(8,128)S(1)} %fusion.7), custom_call_target="Cholesky" | custom-call | tf_op jit(solution)/shard_map/jit(cholesky)/cholesky | solution.py:323
  82.6 0.6 compare_reduce_fusion.1
  83.2 0.6 select_bitcast_fusion.1
  83.8 9.8 %custom-call.6 = f32[1,128,128]{1,2,0:T(8,128)S(1)} custom-call(f32[1,128,128]{2,1,0:T(8,128)S(1)} %select_bitcast_fusion.1), custom_call_target="InvertDiagBlocksLowerTriangular" | custom-call | tf_op jit(solution)/shard_map/jit(_solve_triangular)/triangular_solve | solution.py:325
  93.6 0.3 fusion.2
  93.9 2.4 %fusion.16.matrix = f32[1024,128]{1,0:T(8,128)} fusion(f32[1024,128]{1,0:T(8,128)} %bitcast.30, f32[128,128]{1,0:T(8,128)S(1)} %fusion.2), kind=kOutput, calls=%fused_computation.29 | convolution fusion | flops 201326592 | bytes 1114112 | tf_op jit(solution)/shard_map/dot_general | solution.py:326
  96.3 17.6 %gram.3 = f32[128,128]{1,0:T(8,128)} custom-call(f32[1024,128]{1,0:T(8,128)} %fusion.16.matrix), custom_call_target="tpu_custom_call" | custom-call | tf_op jit(solution)/shard_map/gram/pallas_call | solution.py:306
  113.9 0.9 copy.9
  114.8 0.9 fusion.5
  115.7 11.9 %cholesky.55 = f32[128,128]{1,0:T(8,128)S(1)} custom-call(f32[128,128]{1,0:T(8,128)S(1)} %fusion.5), custom_call_target="Cholesky" | custom-call | tf_op jit(solution)/shard_map/jit(cholesky)/cholesky | solution.py:323
  127.6 0.6 compare_reduce_fusion
  128.3 2.1 %convolution_multiply_fusion.1 = f32[128,128]{1,0:T(8,128)} fusion(f32[128,128]{1,0:T(8,128)S(1)} %cholesky.44, f32[128,128]{1,0:T(8,128)S(1)} %cholesky.55, pred[]{:T(512)} %compare_reduce_fusion, pred[]{:T(512)} %compare_reduce_fusion.1), kind=kOutput, calls=%fused_computation.2 | convolution fusion | flops 25280512 | bytes 196610 | tf_op jit(solution)/shard_map/dot_general | solution.py:339
  130.4 0.7 select_bitcast_fusion
  131.1 9.8 %custom-call.7 = f32[1,128,128]{1,2,0:T(8,128)S(1)} custom-call(f32[1,128,128]{2,1,0:T(8,128)S(1)} %select_bitcast_fusion), custom_call_target="InvertDiagBlocksLowerTriangular" | custom-call | tf_op jit(solution)/shard_map/jit(_solve_triangular)/triangular_solve | solution.py:325
  140.9 0.3 fusion
  141.2 2.4 %convolution_multiply_fusion = f32[1024,128]{1,0:T(8,128)} fusion(f32[1024,128]{1,0:T(8,128)} %fusion.16.matrix, f32[128,128]{1,0:T(8,128)S(1)} %fusion), kind=kOutput, calls=%fused_computation.1 | convolution fusion | flops 201457664 | bytes 1114112 | tf_op jit(solution)/shard_map/dot_general | solution.py:326
  (2 shorter events, 0.1 us)
Async XLA Ops:
  0.6 2.6 %copy-start.2 = (s32[8,128]{1,0:T(8,128)S(1)}, s32[8,128]{1,0:T(8,128)}, u32[]{:S(2)}) copy-start(s32[8,128]{1,0:T(8,128)} %degrees.1) | copy-start | bytes 12292
  0.6 2.6 %copy-start.1 = (f32[8,128,128]{2,1,0:T(8,128)S(1)}, f32[8,128,128]{2,1,0:T(8,128)}, u32[]{:S(2)}) copy-start(f32[8,128,128]{2,1,0:T(8,128)} %start.1) | copy-start | bytes 1572868
  49.0 0.8 copy-start

commit v2 on v1

--- a/solution.py
+++ b/solution.py
@@ -23,7 +23,7 @@
 
 
 def filter_kernel(
-    ra_count, dec_count, offsets, start, edges, degrees, out,
+    ra_count, dec_count, offsets, start, edges, degrees, out, local,
     fields, low, high, left, right, wide, thin, wide_halo, thin_halo, edge_pair, edge_third, degree_cols,
     send_sem, recv_sem,
 ):
@@ -237,6 +237,7 @@
         if version < STEPS - 1:
             start_middle(version + 1)
 
+    local[...] = own_gram(out[...].reshape(rows * 128, 128))
     for version in range(STEPS):
         finish_sends(version)
 
@@ -247,9 +248,9 @@
     depth = 4 * 128 + HALO
     return pl.pallas_call(
         functools.partial(filter_kernel, lax.axis_size("ra"), lax.axis_size("dec")),
-        out_shape=jax.ShapeDtypeStruct(start_block.shape, F32),
+        out_shape=(jax.ShapeDtypeStruct(start_block.shape, F32), jax.ShapeDtypeStruct((128, 128), F32)),
         in_specs=[pl.BlockSpec(memory_space=pltpu.SMEM), vmem, vmem, vmem],
-        out_specs=vmem,
+        out_specs=(vmem, vmem),
         scratch_shapes=[
             pltpu.VMEM((STEPS - 1, rows, 128, 128), F32),
             pltpu.VMEM((STEPS, 2, 128, 128), F32),
@@ -271,73 +272,158 @@
     )(offsets, start_block, edges, degrees)
 
 
-def gram_kernel(ra_count, dec_count, matrix, total, sums, came, send_sem, recv_sem):
+def sum_kernel(ra_count, dec_count, local, total, sums, came, pair_came, send_sem, recv_sem, pair_send, pair_recv):
     ra = lax.axis_index("ra")
     dec = lax.axis_index("dec")
+    side = lax.rem(dec, 2)
+    mine = pl.ds(pl.multiple_of(side * 64, 64), 64)
+    other = pl.ds(pl.multiple_of(64 - side * 64, 64), 64)
+    pair = (ra, dec + 1 - 2 * side)
     partners = []
-    for bit in range(dec_count.bit_length() - 1):
+    for bit in range(1, dec_count.bit_length() - 1):
         step = 2**bit
         partners.append((ra, dec + step - 2 * step * lax.rem(dec // step, 2)))
     for bit in range(ra_count.bit_length() - 1):
         step = 2**bit
         partners.append((ra + step - 2 * step * lax.rem(ra // step, 2), dec))
     barrier = pltpu.get_barrier_semaphore()
-    for partner in partners:
+    for partner in [pair] + partners:
         pl.semaphore_signal(barrier, inc=1, device_id=partner, device_id_type=MESH)
-    local = lax.dot_general(
-        matrix[...], matrix[...], (((0,), (0,)), ((), ())), precision=lax.Precision.HIGHEST, preferred_element_type=F32
-    )
-    pl.semaphore_wait(barrier, len(partners))
+    pl.semaphore_wait(barrier, len(partners) + 1)
+    gather = pltpu.make_async_remote_copy(
+        src_ref=local.at[other], dst_ref=pair_came, send_sem=pair_send.at[0], recv_sem=pair_recv.at[0],
+        device_id=pair, device_id_type=MESH,
+    )
+    gather.start()
+    gather.wait()
+    value = local[mine] + pair_came[...]
     for level, partner in enumerate(partners):
-        sums[level] = local
+        sums[level] = value
         move = pltpu.make_async_remote_copy(
             src_ref=sums.at[level], dst_ref=came.at[level], send_sem=send_sem.at[level], recv_sem=recv_sem.at[level],
             device_id=partner, device_id_type=MESH,
         )
         move.start()
         move.wait()
-        local = local + came[level]
-    total[...] = local
-
-
-def whole_gram(matrix):
+        value = value + came[level]
+    total[mine] = value
+    share = pltpu.make_async_remote_copy(
+        src_ref=total.at[mine], dst_ref=total.at[mine], send_sem=pair_send.at[1], recv_sem=pair_recv.at[1],
+        device_id=pair, device_id_type=MESH,
+    )
+    share.start()
+    share.wait()
+
+
+def sum_over_devices(local):
     vmem = pl.BlockSpec(memory_space=pltpu.VMEM)
-    levels = lax.axis_size(("ra", "dec")).bit_length() - 1
+    levels = lax.axis_size(("ra", "dec")).bit_length() - 2
     return pl.pallas_call(
-        functools.partial(gram_kernel, lax.axis_size("ra"), lax.axis_size("dec")),
+        functools.partial(sum_kernel, lax.axis_size("ra"), lax.axis_size("dec")),
         out_shape=jax.ShapeDtypeStruct((128, 128), F32),
         in_specs=[vmem],
         out_specs=vmem,
         scratch_shapes=[
-            pltpu.VMEM((levels, 128, 128), F32),
-            pltpu.VMEM((levels, 128, 128), F32),
+            pltpu.VMEM((levels, 64, 128), F32),
+            pltpu.VMEM((levels, 64, 128), F32),
+            pltpu.VMEM((64, 128), F32),
             pltpu.SemaphoreType.DMA((levels,)),
             pltpu.SemaphoreType.DMA((levels,)),
+            pltpu.SemaphoreType.DMA((2,)),
+            pltpu.SemaphoreType.DMA((2,)),
         ],
         compiler_params=pltpu.CompilerParams(collective_id=1, has_side_effects=True),
-        name="gram",
-    )(matrix)
-
-
-def cholesky_pass(matrix):
-    lower = jnp.linalg.cholesky(whole_gram(matrix))
-    identity = jnp.eye(matrix.shape[1], dtype=matrix.dtype)
-    inverse_lower = jax.scipy.linalg.solve_triangular(lower, identity, lower=True)
-    ortho = jnp.dot(matrix, inverse_lower.T, precision=lax.Precision.HIGHEST)
-    return (ortho, lower.T)
+        name="sum_gram",
+    )(local)
+
+
+def factor(gram):
+    tile = (8, 128)
+    sub = lax.broadcasted_iota(jnp.int32, tile, 0)
+    lane = lax.broadcasted_iota(jnp.int32, tile, 1)
+    blocks = 16
+    gram = 0.5 * (gram + gram.T)
+    body = [gram[8 * m : 8 * m + 8] for m in range(blocks)]
+    side = [jnp.where(lane == sub + 8 * m, 1.0, 0.0).astype(F32) for m in range(blocks)]
+    upper, inverse = [], []
+
+    def row_of(value, i):
+        return jnp.broadcast_to(value[i : i + 1], tile)
+
+    for k in range(blocks):
+        columns = {
+            m: [jnp.broadcast_to(body[m][:, 8 * k + i : 8 * k + i + 1], tile) for i in range(8)] for m in range(k, blocks)
+        }
+        left, right = body[k], side[k]
+        upper_rows, inverse_rows = left, right
+        left_rows, right_rows = [], []
+        for i in range(8):
+            pivot = row_of(columns[k][i], i)
+            root = lax.rsqrt(pivot)
+            root = root * (1.5 - 0.5 * pivot * root * root)
+            entries = [row_of(columns[k][j], i) * root for j in range(i + 1, 8)]
+            for m in range(k, blocks):
+                columns[m][i] = columns[m][i] * root
+                for j in range(i + 1, 8):
+                    columns[m][j] = columns[m][j] - columns[m][i] * entries[j - i - 1]
+            left_row, right_row = row_of(left, i) * root, row_of(right, i) * root
+            left_rows.append(left_row)
+            right_rows.append(right_row)
+            upper_rows = jnp.where(sub == i, left_row, upper_rows)
+            inverse_rows = jnp.where(sub == i, right_row, inverse_rows)
+            left = left - columns[k][i] * left_row
+            right = right - columns[k][i] * right_row
+        upper.append(jnp.where(lane >= sub + 8 * k, upper_rows, 0.0))
+        inverse.append(jnp.where(lane <= sub + 8 * k, inverse_rows, 0.0))
+        for m in range(k + 1, blocks):
+            for i in range(8):
+                body[m] = body[m] - columns[m][i] * left_rows[i]
+                side[m] = side[m] - columns[m][i] * right_rows[i]
+    return jnp.concatenate(upper, axis=0), jnp.concatenate(inverse, axis=0)
+
+
+def own_gram(matrix):
+    return lax.dot_general(
+        matrix, matrix, (((0,), (0,)), ((), ())), precision=lax.Precision.HIGHEST, preferred_element_type=F32
+    )
+
+
+def times_transposed(matrix, inverse):
+    return lax.dot_general(
+        matrix, inverse, (((1,), (1,)), ((), ())), precision=lax.Precision.HIGHEST, preferred_element_type=F32
+    )
+
+
+def first_kernel(gram, matrix, ortho, upper, local):
+    upper[...], inverse = factor(gram[...])
+    value = times_transposed(matrix[...], inverse)
+    ortho[...] = value
+    local[...] = own_gram(value)
+
+
+def second_kernel(scale, gram, matrix, upper_first, basis, rfactor):
+    upper, inverse = factor(gram[...])
+    basis[...] = times_transposed(matrix[...], inverse) * scale
+    rfactor[...] = jnp.dot(upper, upper_first[...], precision=lax.Precision.HIGHEST, preferred_element_type=F32) / scale
 
 
 def on_device(start_block, edge_blocks, block_offsets, degree_counts):
-    current = filtered_field(start_block, edge_blocks[:, 0], block_offsets[:, 0], degree_counts)
+    current, local = filtered_field(start_block, edge_blocks[:, 0], block_offsets[:, 0], degree_counts)
     row_count, node_count, column_count = current.shape
     filtered = current.reshape(row_count * node_count, column_count)
-    ortho_first, upper_first = cholesky_pass(filtered)
-    ortho_second, upper_second = cholesky_pass(ortho_first)
     total_nodes = row_count * node_count * lax.axis_size("ra") * lax.axis_size("dec")
-    scale = jnp.sqrt(jnp.asarray(total_nodes, dtype=jnp.float32))
-    basis = (ortho_second * scale).reshape(row_count, node_count, column_count)
-    rfactor = jnp.dot(upper_second, upper_first, precision=lax.Precision.HIGHEST) / scale
-    return (basis, rfactor)
+    scale = total_nodes**0.5
+    vmem = pl.BlockSpec(memory_space=pltpu.VMEM)
+    tall = jax.ShapeDtypeStruct(filtered.shape, F32)
+    square = jax.ShapeDtypeStruct((128, 128), F32)
+    ortho, upper_first, local = pl.pallas_call(
+        first_kernel, out_shape=(tall, square, square), in_specs=[vmem] * 2, out_specs=(vmem,) * 3, name="first_pass"
+    )(sum_over_devices(local), filtered)
+    basis, rfactor = pl.pallas_call(
+        functools.partial(second_kernel, scale), out_shape=(tall, square), in_specs=[vmem] * 3, out_specs=(vmem,) * 2,
+        name="second_pass",
+    )(sum_over_devices(local), ortho, upper_first)
+    return (basis.reshape(current.shape), rfactor)
 
 
 def solution(mesh):

time: 144 us -> 102 us (0.71)
  other arithmetic: 47.5 us -> 0 us
  Pallas kernels: 82.6 us -> 96.9 us
  matrix products: 7.52 us -> 0 us
    another operation x10 -> x0, other arithmetic: 45.8 us -> none  [the longest x6 25 us: cholesky_pass(): lower = jnp.linalg.cholesky(whole_gram(matrix))]
    pallas_call x2 -> x4, Pallas kernels: 36.8 us -> 50.5 us  [the longest x2 34.2 us: sum_over_devices(): pl.pallas_call(functools.partial(sum_kernel, lax.axis_size('ra'), lax.axi...]
    dot_general x3 -> x0, matrix products: 6.95 us -> none  [the longest x2 4.83 us: cholesky_pass(): ortho = jnp.dot(matrix, inverse_lower.T, precision=lax.Precision.HIGHEST)]
    pallas_call x2 -> x0, local copies, waits for them, and re-layouts: 1.85 us -> none  [whole_gram(): pl.pallas_call(functools.partial(gram_kernel, lax.axis_size('ra'), lax.ax...]
    div x2 -> x0, other arithmetic: 1.71 us -> none  [cholesky_pass(): lower = jnp.linalg.cholesky(whole_gram(matrix))]
    unnamed x7 -> x9, local copies, waits for them, and re-layouts: 2.56 us -> 3.19 us
where the time goes in v2:
time: 102 us
  Pallas kernels  96.9 us (95%)
  local copies, waits for them, and re-layouts  4 us (4%)
    pallas_call x1, Pallas kernels, filtered_field(): pl.pallas_call(functools.partial(filter_kernel, lax.axis_size('ra'), lax....  46.4 us
    pallas_call x2, Pallas kernels, sum_over_devices(): pl.pallas_call(functools.partial(sum_kernel, lax.axis_size('ra'), lax.axi...  34.2 us
    pallas_call x1, Pallas kernels, on_device(): pl.pallas_call(first_kernel, out_shape=(tall, square, square), in_specs=[...  8.7 us
    pallas_call x1, Pallas kernels, on_device(): pl.pallas_call(functools.partial(second_kernel, scale), out_shape=(tall,...  7.63 us
    unnamed x9, local copies, waits for them, and re-layouts  3.19 us

profile of v2, /device:TPU:0, one launch (start us, length us, event | category | flops | bytes accessed | tf_op | source)
XLA Modules:
  0.0 101.6 jit_solution(17182034615255798598)
XLA Ops:
  0.6 0.0 copy-start.3
  0.6 0.0 copy-start.1
  0.6 0.8 copy.7.offsets
  1.5 1.8 %copy.9 = f32[8,1,4,132,128]{4,3,2,0,1:T(8,128)S(1)} copy(f32[8,1,4,132,128]{4,2,3,1,0:T(4,128)} %param.5) | data formatting | bytes 4325376 | tf_op args[1]
  3.2 0.0 copy-done.3
  3.2 0.0 copy-done.1
  3.2 46.4 %filter.1 = (f32[8,128,128]{2,1,0:T(8,128)S(1)}, f32[128,128]{1,0:T(8,128)S(1)}) custom-call(s32[8,4]{1,0:T(8,128)S(1)} %copy.7.offsets, f32[8,128,128]{2,1,0:T(8,128)S(1)} %copy-done.1, f32[8,4,132,128]{3,2,1,0:T(8,128)S(1)} %bitcast.6, s32[8,128]{1,0:T(8,128)S(1)} %copy-done.3), custom_call_target="tpu_custom_call" | custom-call | tf_op jit(solution)/shard_map/filter/pallas_call | solution.py:249
  49.7 0.0 copy-start
  49.7 0.8 copy-done
  50.5 0.0 copy-start.2
  50.5 0.6 copy-done.2
  51.1 17.6 %sum_gram.2.gram = f32[128,128]{1,0:T(8,128)} custom-call(f32[128,128]{1,0:T(8,128)} %copy-done.2), custom_call_target="tpu_custom_call" | custom-call | tf_op jit(solution)/shard_map/sum_gram/pallas_call | solution.py:321
  68.8 8.7 %first_pass.1 = (f32[1024,128]{1,0:T(8,128)}, f32[128,128]{1,0:T(8,128)}, f32[128,128]{1,0:T(8,128)}) custom-call(f32[128,128]{1,0:T(8,128)} %sum_gram.2.gram, f32[1024,128]{1,0:T(8,128)} %bitcast.7), custom_call_target="tpu_custom_call" | custom-call | tf_op jit(solution)/shard_map/first_pass/pallas_call | solution.py:419
  77.5 16.5 %sum_gram.3.gram = f32[128,128]{1,0:T(8,128)} custom-call(f32[128,128]{1,0:T(8,128)} %get-tuple-element.11.local), custom_call_target="tpu_custom_call" | custom-call | tf_op jit(solution)/shard_map/sum_gram/pallas_call | solution.py:321
  94.0 7.6 %second_pass.1 = (f32[1024,128]{1,0:T(8,128)}, f32[128,128]{1,0:T(8,128)}) custom-call(f32[128,128]{1,0:T(8,128)} %sum_gram.3.gram, f32[1024,128]{1,0:T(8,128)} %get-tuple-element.12.matrix, f32[128,128]{1,0:T(8,128)} %get-tuple-element.13.upper_first), custom_call_target="tpu_custom_call" | custom-call | tf_op jit(solution)/shard_map/second_pass/pallas_call | solution.py:422
Async XLA Ops:
  0.6 2.6 %copy-start.3 = (s32[8,128]{1,0:T(8,128)S(1)}, s32[8,128]{1,0:T(8,128)}, u32[]{:S(2)}) copy-start(s32[8,128]{1,0:T(8,128)} %degrees.1) | copy-start | bytes 12292
  0.6 2.6 %copy-start.1 = (f32[8,128,128]{2,1,0:T(8,128)S(1)}, f32[8,128,128]{2,1,0:T(8,128)}, u32[]{:S(2)}) copy-start(f32[8,128,128]{2,1,0:T(8,128)} %start.1) | copy-start | bytes 1572868
  49.7 0.8 copy-start
  50.5 0.6 copy-start.2
